TPU v7x, 256 devices: a whole 4x4x8 slice. The times are simulated.
256 devices in a mesh: req: 32 (over z, y), tp: 8 (over x, core).
Axes of the slice: x: 4, y: 4, z: 8, core: 2. Of those that a mesh axis runs over, the one named last changes fastest.
Arguments:
- hidden: bfloat16 [9472, 5120], P('req', 'tp'), may hold values from -6 to 6
- raw_q: bfloat16 [9472, 3072], P('req', 'tp'), may hold values from -70 to 70
- raw_k: bfloat16 [9472, 3072], P('req', 'tp'), may hold values from -70 to 70
- raw_v: bfloat16 [9472, 3072], P('req', 'tp'), may hold values from -6 to 6
- q_gain: float32 [3072], P('tp'), may hold values from 0.5 to 2
- k_gain: float32 [3072], P('tp'), may hold values from 0.5 to 2
- out_weight: bfloat16 [3072, 5120], P('tp'), may hold values from -0.109375 to 0.109375
- post_gain: float32 [5120], P('tp'), may hold values from 0.25 to 1.75
- prefix_keys: bfloat16 [32, 32, 128, 3072], P(None, 'req', None, 'tp'), may hold values from -420 to 420
- prefix_values: bfloat16 [32, 32, 128, 3072], P(None, 'req', None, 'tp'), may hold values from -6 to 6
- key_cache: bfloat16 [256, 128, 3072], P('req', None, 'tp'), may hold values from -420 to 420
- value_cache: bfloat16 [256, 128, 3072], P('req', None, 'tp'), may hold values from -6 to 6
- slot_owner: int32 [256], P('req'), may hold values from -1 to 255, as said below
- slot_page: int32 [256], P('req'), may hold values from 0 to 127, as said below
- cache_lengths: int32 [256], replicated, may hold values from 0 to 16384, as said below
- span_offsets: int32 [32], replicated, may hold values from 0 to 4096
Outputs:
- new_hidden: bfloat16 [9472, 5120], P('req', 'tp')
Inputs may be any that keep to these rules, and one draw needn't show every extreme that they name: Each pool slot holds one page of decode request slot_owner[s], or nothing where it is -1. No page of a request is held twice, and a request holding c pages holds pages 0 to c - 1. `slot_page`: 0 for a slot that holds nothing. `cache_lengths`: A request holding c pages of the pool has a length from (c - 1) * 128 + 1 to c * 128, and 0 where c = 0.
All inputs are finite; a program needn't handle non-finite values.
Results may differ from a plain program's by a relative error of at most 0.0076.
Values may be sent and summed in bfloat16 or wider, within the bound.
A program may use at most 128 MiB of HBM per device.

v0:
```python
import jax
import jax.numpy as jnp
from jax import lax
from jax.sharding import PartitionSpec as P

HD = 128
SPAN = 288
DEC = 8
EPSILON = 1e-06
THETA = 500000.0
NEGATIVE = -1e30


def rotate(values, positions):
    half_width = values.shape[-1] // 2
    frequency = THETA ** (-(jnp.arange(half_width, dtype=jnp.float32) * 2.0 / values.shape[-1]))
    angles = positions.astype(jnp.float32)[:, None] * frequency[None, :]
    cosine = jnp.cos(angles)[:, None, :]
    sine_part = jnp.sin(angles)[:, None, :]
    first_half = values[..., :half_width]
    second = values[..., half_width:]
    return jnp.concatenate(
        [first_half * cosine - second * sine_part, second * cosine + first_half * sine_part], -1
    )


def softmax_part(scores, key_mask, values, form):
    masked = jnp.where(key_mask, scores, NEGATIVE)
    top_score = jnp.max(masked, -1)
    exp_terms = jnp.where(key_mask, jnp.exp(masked - top_score[..., None]), 0.0)
    weight_sum = jnp.sum(exp_terms, -1)
    numerator = jnp.einsum(
        form, exp_terms.astype(jnp.bfloat16), values, preferred_element_type=jnp.float32
    )
    return (top_score, weight_sum, numerator)


def merge_parts(top_scores, weight_sums, numerators):
    best_score = jnp.max(top_scores, 0)
    factor = jnp.exp(top_scores - best_score[None])
    weight_sum = jnp.sum(factor * weight_sums, 0)
    numerator = jnp.sum(factor[..., None] * numerators, 0)
    return numerator / weight_sum[..., None]


def body(
    hidden,
    raw_q,
    raw_k,
    raw_v,
    q_gain,
    k_gain,
    out_weight,
    post_gain,
    prefix_keys,
    prefix_values,
    key_cache,
    value_cache,
    slot_owner,
    slot_page,
    cache_lengths,
    span_offsets,
):
    groups = lax.axis_size("req")
    my_group = lax.axis_index("req")
    tp_count = lax.axis_size("tp")
    tp_index = lax.axis_index("tp")
    rows_group = SPAN + DEC
    local_width = raw_q.shape[1]
    local_heads = local_width // HD
    requests = groups * DEC
    score_scale = HD ** (-0.5)
    page_rows = key_cache.shape[1]
    own_lengths = lax.dynamic_slice_in_dim(cache_lengths, my_group * DEC, DEC)
    positions = jnp.concatenate(
        [span_offsets[my_group] + jnp.arange(SPAN, dtype=jnp.int32), own_lengths]
    )
    float_query = raw_q.astype(jnp.float32)
    float_key = raw_k.astype(jnp.float32)
    query_power, key_power = lax.psum(
        (jnp.sum(float_query * float_query, 1), jnp.sum(float_key * float_key, 1)), "tp"
    )
    full_width = local_width * tp_count
    normed_query = (
        float_query * lax.rsqrt(query_power / full_width + EPSILON)[:, None] * q_gain[None, :]
    )
    normed_key = float_key * lax.rsqrt(key_power / full_width + EPSILON)[:, None] * k_gain[None, :]
    query = rotate(normed_query.reshape(rows_group, local_heads, HD), positions).astype(
        jnp.bfloat16
    )
    key_rows = rotate(normed_key.reshape(rows_group, local_heads, HD), positions).astype(
        jnp.bfloat16
    )
    value_rows = raw_v.reshape(rows_group, local_heads, HD)
    causal = jnp.arange(SPAN)[:, None] >= jnp.arange(SPAN)[None, :]
    self_scores = (
        jnp.einsum(
            "qhd,khd->qhk", query[:SPAN], key_rows[:SPAN], preferred_element_type=jnp.float32
        )
        * score_scale
    )
    self_top, self_total, self_numerator = softmax_part(
        self_scores, causal[:, None, :], value_rows[:SPAN], "qhk,khd->qhd"
    )
    own_scores = (
        jnp.sum(query[SPAN:].astype(jnp.float32) * key_rows[SPAN:].astype(jnp.float32), -1)
        * score_scale
    )
    own_total = jnp.ones_like(own_scores)
    own_numerator = value_rows[SPAN:].astype(jnp.float32)
    everyone = lax.all_gather(query, "req", axis=0, tiled=True)
    everyone = everyone.reshape(groups, rows_group, local_heads, HD)
    pages_here = prefix_keys.shape[1]
    block_keys = prefix_keys.reshape(groups, pages_here * page_rows, local_heads, HD)
    block_values = prefix_values.reshape(groups, pages_here * page_rows, local_heads, HD)
    key_pos = my_group * pages_here * page_rows + jnp.arange(
        pages_here * page_rows, dtype=jnp.int32
    )
    key_mask = key_pos[None, :] < span_offsets[:, None]
    scores = (
        jnp.einsum(
            "gqhd,gkhd->gqhk", everyone[:, :SPAN], block_keys, preferred_element_type=jnp.float32
        )
        * score_scale
    )
    pre_top, pre_total, pre_numerator = softmax_part(
        scores, key_mask[:, None, None, :], block_values, "gqhk,gkhd->gqhd"
    )
    live_slot = slot_owner >= 0
    owner_index = jnp.maximum(slot_owner, 0)
    slot_queries = everyone[:, SPAN:].reshape(requests, local_heads, HD)[owner_index]
    slot_keys = key_cache.reshape(key_cache.shape[0], page_rows, local_heads, HD)
    slot_values = value_cache.reshape(value_cache.shape[0], page_rows, local_heads, HD)
    scores = (
        jnp.einsum("shd,sphd->shp", slot_queries, slot_keys, preferred_element_type=jnp.float32)
        * score_scale
    )
    key_pos = slot_page[:, None] * page_rows + jnp.arange(page_rows, dtype=jnp.int32)[None, :]
    key_mask = live_slot[:, None] & (key_pos < cache_lengths[owner_index][:, None])
    top_score, weight_sum, numerator = softmax_part(
        scores, key_mask[:, None, :], slot_values, "shp,sphd->shd"
    )
    member = slot_owner[None, :] == jnp.arange(requests, dtype=jnp.int32)[:, None]
    best_score = jnp.max(jnp.where(member[:, :, None], top_score[None], NEGATIVE), 1)
    factor = jnp.where(member[:, :, None], jnp.exp(top_score[None] - best_score[:, None]), 0.0)
    request_total = jnp.einsum("rsh,sh->rh", factor, weight_sum, precision=lax.Precision.HIGHEST)
    request_numerator = jnp.einsum(
        "rsh,shd->rhd", factor, numerator, precision=lax.Precision.HIGHEST
    )
    send_top = jnp.concatenate([pre_top, best_score.reshape(groups, DEC, local_heads)], 1).reshape(
        groups * rows_group, local_heads
    )
    send_total = jnp.concatenate(
        [pre_total, request_total.reshape(groups, DEC, local_heads)], 1
    ).reshape(groups * rows_group, local_heads)
    send_numerator = jnp.concatenate(
        [pre_numerator, request_numerator.reshape(groups, DEC, local_heads, HD)], 1
    ).reshape(groups * rows_group, local_heads, HD)
    back_top, back_total, back_numerator = (
        lax.all_to_all(send_top, "req", split_axis=0, concat_axis=0, tiled=True),
        lax.all_to_all(send_total, "req", split_axis=0, concat_axis=0, tiled=True),
        lax.all_to_all(send_numerator, "req", split_axis=0, concat_axis=0, tiled=True),
    )
    local_top = jnp.concatenate([self_top, own_scores], 0)
    local_total = jnp.concatenate([self_total, own_total], 0)
    local_numerator = jnp.concatenate([self_numerator, own_numerator], 0)
    merged = merge_parts(
        jnp.concatenate([back_top.reshape(groups, rows_group, local_heads), local_top[None]], 0),
        jnp.concatenate(
            [back_total.reshape(groups, rows_group, local_heads), local_total[None]], 0
        ),
        jnp.concatenate(
            [back_numerator.reshape(groups, rows_group, local_heads, HD), local_numerator[None]], 0
        ),
    )
    attention = merged.reshape(rows_group, local_width).astype(jnp.bfloat16)
    share_width = post_gain.shape[0]
    projected = lax.psum(jnp.dot(attention, out_weight, preferred_element_type=jnp.float32), "tp")
    inverse = lax.rsqrt(jnp.mean(projected * projected, 1) + EPSILON)
    my_share = lax.dynamic_slice_in_dim(projected, tp_index * share_width, share_width, 1)
    normed = my_share * inverse[:, None]
    return (hidden.astype(jnp.float32) + normed * post_gain[None, :]).astype(jnp.bfloat16)


def solution(mesh):
    return jax.shard_map(
        body,
        mesh=mesh,
        in_specs=(
            P("req", "tp"),
            P("req", "tp"),
            P("req", "tp"),
            P("req", "tp"),
            P("tp"),
            P("tp"),
            P("tp", None),
            P("tp"),
            P(None, "req", None, "tp"),
            P(None, "req", None, "tp"),
            P("req", None, "tp"),
            P("req", None, "tp"),
            P("req"),
            P("req"),
            P(),
            P(),
        ),
        out_specs=P("req", "tp"),
        check_vma=False,
    )
```

profile of v0, /device:TPU:1, one launch (start us, length us, event | category | flops | bytes accessed | tf_op | source)
XLA Modules:
  0.0 842.2 jit_solution(3925593860115718974)
XLA Ops:
  6.6 1.2 dynamic_slice.9
  7.8 0.6 iota_add_fusion
  8.5 1.1 fusion.22
  9.5 1.1 fusion.24
  10.6 15.0 %all-reduce.1 = (f32[296]{0:T(512)S(1)}, f32[296]{0:T(512)S(1)}) all-reduce(f32[296]{0:T(512)S(1)} %fusion.24, f32[296]{0:T(512)S(1)} %fusion.22), channel_id=1, replica_groups=mesh['req'=32,'tp'=8] {'tp'}, use_global_device_ids=true, to_apply=%region_6.7 | all-reduce | flops 592 | bytes 4736 | tf_op jit(solution)/shard_map/psum | solution.py:80
  25.6 1.1 fusion.25
  26.7 0.2 reshape.278
  26.9 1.0 fusion.23
  27.9 0.2 reshape.272
  28.1 1.4 fusion.74
  29.5 1.5 fusion.75
  31.0 0.1 dynamic_slice.10
  31.1 0.1 add_convert_fusion.3
  31.1 0.6 multiply_cosine_fusion
  31.7 2.8 subtract_convert_fusion.1
  34.6 0.7 copy-done.4
  35.2 0.1 copy-done.6
  35.3 0.8 pad_maximum_fusion.3
  36.2 0.6 gather_fusion
  36.8 2.3 copy.97
  39.2 2.3 copy.104
  41.5 2.9 copy.94
  44.4 3.5 copy.102
  47.9 0.1 iota_compare_fusion.1
  48.0 0.1 fusion.62
  48.1 81.2 %all-gather.2.cloned.1.call-done = bf16[9472,3,128]{2,0,1:T(8,128)(2,1)} async-done(((bf16[296,3,128]{2,0,1:T(8,128)(2,1)}), bf16[9472,3,128]{2,0,1:T(8,128)(2,1)}) %all-gather.2.cloned.1.call-update) | async-done | bytes 7274512 | tf_op jit(solution)/shard_map/all_gather | solution.py:111
  129.3 0.9 slice_bitcast_fusion.1
  130.3 0.2 copy.96
  130.5 0.6 gather_fusion.1
  131.0 1.4 fusion.47
  132.5 0.1 fusion.59
  132.6 0.8 fusion.57
  133.3 0.1 select_reduce_fusion
  133.4 0.1 reshape.277
  133.6 1.6 fusion.45
  135.2 1.3 convolution_bitcast_fusion.2
  136.5 14.0 %bitcast_reduce_fusion = (f32[32,288,3]{1,2,0:T(4,128)S(1)}, f32[32,3,288,128]{3,2,1,0:T(8,128)}) fusion(pred[32,128]{1,0:T(8,128)(4,1)S(1)} %broadcast_compare_fusion, bf16[32,128,3,128]{1,3,2,0:T(8,128)(2,1)} %bitcast.96, bf16[32,296,3,128]{3,1,0,2:T(8,128)(2,1)} %bitcast.102), kind=kOutput, calls=%fused_computation.6 | convolution fusion | flops 916558848 | bytes 24494080 | tf_op jit(solution)/shard_map/gqhd,gkhd->gqhk/dot_general | solution.py:121
  150.5 0.8 pad_maximum_fusion.1
  151.3 5.8 all-to-all-start
  157.1 11.8 %fusion.3 = f32[32,288,3]{1,2,0:T(4,128)} fusion(f32[32,3,288,128]{3,2,1,0:T(8,128)} %get-tuple-element.28, f32[32,288,3]{1,2,0:T(4,128)S(1)} %get-tuple-element.27, pred[32,128]{1,0:T(8,128)(4,1)S(1)} %broadcast_compare_fusion), kind=kLoop, calls=%fused_computation.10 | loop fusion | flops 17667072 | bytes 14381056 | tf_op jit(solution)/shard_map/reduce_sum | solution.py:31
  168.9 10.0 %convolution_bitcast_fusion = f32[32,288,3,128]{3,1,2,0:T(8,128)} fusion(bf16[32,128,3,128]{1,3,2,0:T(8,128)(2,1)S(1)} %bitcast.95, f32[32,3,288,128]{3,2,1,0:T(8,128)S(1)} %copy-done.1, f32[32,288,3]{1,2,0:T(4,128)S(1)} %get-tuple-element.27, pred[32,128]{1,0:T(8,128)(4,1)S(1)} %broadcast_compare_fusion), kind=kOutput, calls=%fused_computation.12 | convolution fusion | flops 923664384 | bytes 31571968 | tf_op jit(solution)/shard_map/gqhk,gkhd->gqhd/dot_general | solution.py:32
  178.8 0.2 fusion.41
  179.1 0.1 reshape.284
  179.2 1.2 copy.105
  180.4 1.7 pad_maximum_fusion.2
  182.1 9.0 %all-to-all-start.2 = ((f32[32,296,3]{1,2,0:T(4,128)}), f32[32,296,3]{1,2,0:T(4,128)S(1)}, u32[]{:S(2)}, u32[]{:S(2)}) async-start(f32[32,296,3]{1,2,0:T(4,128)} %pad_maximum_fusion.2), calls=%async_computation.2 | async-start | bytes 393216 | tf_op jit(solution)/shard_map/all_to_all | solution.py:161
  191.2 11.1 %pad_maximum_fusion = f32[32,296,3,128]{3,1,2,0:T(8,128)} fusion(f32[32,288,3,128]{3,1,2,0:T(8,128)} %convolution_bitcast_fusion, f32[256,3,128]{2,0,1:T(8,128)S(1)} %copy.105), kind=kLoop, calls=%fused_computation.4 | loop fusion | flops 3637248 | bytes 29097984 | tf_op jit(solution)/shard_map/concatenate | solution.py:156
  202.3 11.1 %copy.107 = f32[32,296,3,128]{3,1,0,2:T(8,128)} copy(f32[32,296,3,128]{3,1,2,0:T(8,128)} %pad_maximum_fusion) | data formatting | bytes 29097984 | tf_op jit(solution)/shard_map/concatenate | solution.py:156
  213.4 35.5 %copy.108 = f32[9472,3,128]{2,1,0:T(4,128)} copy(f32[9472,3,128]{2,0,1:T(8,128)} %bitcast.94) | data formatting | bytes 29097984 | tf_op jit(solution)/shard_map/reshape | solution.py:158
  249.0 9.5 %all-to-all-start.1 = ((f32[9472,3,128]{2,1,0:T(4,128)}), f32[9472,3,128]{2,1,0:T(4,128)}, u32[]{:S(2)}, u32[]{:S(2)}) async-start(f32[9472,3,128]{2,1,0:T(4,128)} %copy.108), calls=%async_computation.1 | async-start | bytes 38797312 | tf_op jit(solution)/shard_map/all_to_all | solution.py:162
  258.4 0.3 all-reduce.4.cloned.1.call-start
  258.8 0.2 multiply_reduce_fusion.1
  259.0 0.5 fusion.76
  259.4 0.3 fusion.16
  259.8 0.5 convolution_bitcast_fusion.1
  260.4 0.1 fusion.64
  260.5 0.1 fusion.38
  260.6 449.8 %all-to-all-done.1 = f32[9472,3,128]{2,1,0:T(4,128)} async-done(((f32[9472,3,128]{2,1,0:T(4,128)}), f32[9472,3,128]{2,1,0:T(4,128)}, u32[]{:S(2)}, u32[]{:S(2)}) %all-to-all-start.1) | async-done | bytes 14549024 | tf_op jit(solution)/shard_map/all_to_all | solution.py:162
  710.5 8.4 copy.111
  718.8 4.9 fusion
  723.8 4.4 fusion.26
  728.3 101.8 %all-reduce.4.cloned.1.call-done = f32[296,5120]{1,0:T(8,128)} async-done(((f32[296,5120]{1,0:T(8,128)}), f32[296,5120]{1,0:T(8,128)}) %all-reduce.4.cloned.1.call-update) | async-done | bytes 6062096 | tf_op jit(solution)/shard_map/psum | solution.py:178
  830.1 3.2 multiply_reduce_fusion
  833.3 2.1 add_convert_fusion
  (56 shorter events, 0.5 us)
Async XLA Ops:
  6.5 24.5 %copy-start = (s32[256]{0:T(256)S(1)}, s32[256]{0:T(256)}, u32[]{:S(2)}) copy-start(s32[256]{0:T(256)} %param.30) | copy-start | bytes 3076
  6.5 29.6 %copy-start.13 = (s32[8]{0:T(128)S(1)}, s32[8]{0:T(128)}, u32[]{:S(2)}) copy-start(s32[8]{0:T(128)} %param.28) | copy-start | bytes 100
  6.5 122.8 %all-gather.2.cloned.1.call-start = ((), (), s32[]{:S(2)}) async-start(), calls=%async_computation.3 | async-start | bytes 7501824 | tf_op jit(solution)/shard_map/all_gather | solution.py:111
  31.0 10.5 %copy-start.3 = (bf16[32,1,128,384]{3,2,1,0:T(8,128)(2,1)S(1)}, bf16[32,1,128,384]{3,2,1,0:T(8,128)(2,1)}, u32[]{:S(2)}) copy-start(bf16[32,1,128,384]{3,2,1,0:T(8,128)(2,1)} %param.24) | copy-start | bytes 9437188
  34.6 0.7 copy-start.4
  34.6 0.8 copy-start.6
  39.2 8.7 %copy-start.16 = (s32[8]{0:T(128)S(1)}, s32[8]{0:T(128)}, u32[]{:S(2)}) copy-start(s32[8]{0:T(128)} %param.29) | copy-start | bytes 100
  39.2 8.9 %copy-start.14 = (s32[32]{0:T(128)S(1)}, s32[32]{0:T(128)}, u32[]{:S(2)}) copy-start(s32[32]{0:T(128)} %param.31) | copy-start | bytes 388
  151.3 30.8 %all-to-all-start = ((f32[32,296,3]{1,2,0:T(4,128)}), f32[32,296,3]{1,2,0:T(4,128)S(1)}, u32[]{:S(2)}, u32[]{:S(2)}) async-start(f32[32,296,3]{1,2,0:T(4,128)} %pad_maximum_fusion.1), calls=%async_computation | async-start | bytes 393216 | tf_op jit(solution)/shard_map/all_to_all | solution.py:160
  157.0 11.8 %copy-start.1 = (f32[32,3,288,128]{3,2,1,0:T(8,128)S(1)}, f32[32,3,288,128]{3,2,1,0:T(8,128)}, u32[]{:S(2)}) copy-start(f32[32,3,288,128]{3,2,1,0:T(8,128)} %get-tuple-element.28) | copy-start | bytes 42467332
  168.9 10.0 %copy-start.12 = (f32[8,3]{0,1:T(4,128)S(1)}, f32[8,3]{0,1:T(4,128)}, u32[]{:S(2)}) copy-start(f32[8,3]{0,1:T(4,128)} %get-tuple-element.19) | copy-start | bytes 292
  182.1 66.9 %all-to-all-start.2 = ((f32[32,296,3]{1,2,0:T(4,128)}), f32[32,296,3]{1,2,0:T(4,128)S(1)}, u32[]{:S(2)}, u32[]{:S(2)}) async-start(f32[32,296,3]{1,2,0:T(4,128)} %pad_maximum_fusion.2), calls=%async_computation.2 | async-start | bytes 393216 | tf_op jit(solution)/shard_map/all_to_all | solution.py:161
  248.9 9.8 %copy-start.5 = (bf16[296,3,64]{2,0,1:T(8,128)(2,1)S(1)}, bf16[296,3,64]{2,0,1:T(8,128)(2,1)}, u32[]{:S(2)}) copy-start(bf16[296,3,64]{2,0,1:T(8,128)(2,1)} %copy-done.4) | copy-start | bytes 340996
  248.9 9.8 %copy-start.7 = (bf16[296,3,64]{2,0,1:T(8,128)(2,1)S(1)}, bf16[296,3,64]{2,0,1:T(8,128)(2,1)}, u32[]{:S(2)}) copy-start(bf16[296,3,64]{2,0,1:T(8,128)(2,1)} %copy-done.6) | copy-start | bytes 340996
  248.9 9.8 %copy-start.8 = (bf16[296,3,64]{2,0,1:T(8,128)(2,1)S(1)}, bf16[296,3,64]{2,0,1:T(8,128)(2,1)}, u32[]{:S(2)}) copy-start(bf16[296,3,64]{2,0,1:T(8,128)(2,1)} %get-tuple-element.17) | copy-start | bytes 340996
  248.9 9.8 %copy-start.9 = (bf16[296,3,64]{2,0,1:T(8,128)(2,1)S(1)}, bf16[296,3,64]{2,0,1:T(8,128)(2,1)}, u32[]{:S(2)}) copy-start(bf16[296,3,64]{2,0,1:T(8,128)(2,1)} %get-tuple-element.18) | copy-start | bytes 340996
  248.9 10.8 %copy-start.15 = (bf16[296,384]{1,0:T(8,128)(2,1)S(1)}, bf16[296,384]{1,0:T(8,128)(2,1)}, u32[]{:S(2)}) copy-start(bf16[296,384]{1,0:T(8,128)(2,1)} %param.19) | copy-start | bytes 681988
  249.0 461.5 %all-to-all-start.1 = ((f32[9472,3,128]{2,1,0:T(4,128)}), f32[9472,3,128]{2,1,0:T(4,128)}, u32[]{:S(2)}, u32[]{:S(2)}) async-start(f32[9472,3,128]{2,1,0:T(4,128)} %copy.108), calls=%async_computation.1 | async-start | bytes 38797312 | tf_op jit(solution)/shard_map/all_to_all | solution.py:162
  258.4 571.6 %all-reduce.4.cloned.1.call-start = ((), (), s32[]{:S(2)}) async-start(), calls=%async_computation.4 | async-start | bytes 12124160 | tf_op jit(solution)/shard_map/psum | solution.py:178
  718.8 5.0 copy-start.2
  728.2 105.0 %copy-start.10 = (bf16[296,640]{1,0:T(8,128)(2,1)S(1)}, bf16[296,640]{1,0:T(8,128)(2,1)}, u32[]{:S(2)}) copy-start(bf16[296,640]{1,0:T(8,128)(2,1)} %param.16) | copy-start | bytes 1136644
  728.2 105.0 %copy-start.11 = (f32[640]{0:T(1024)S(1)}, f32[640]{0:T(1024)}, u32[]{:S(2)}) copy-start(f32[640]{0:T(1024)} %param.23) | copy-start | bytes 7684
Sparse Core Ops, SparseCore 0:
  36.3 93.0 all-gather.1
  728.4 101.6 all-reduce.3
where the time goes:
time: 843 us; the launch traced here: 842 us
  waiting for transfers between devices  633 us (75%)
  local copies, waits for them, and re-layouts  75.1 us (9%)
  other arithmetic  46.9 us (6%)
  matrix products  34 us (4%)
  starting transfers between devices  24.5 us (3%)
  blocking collectives  15 us (2%)
  between operations  13.8 us (2%)
    all_to_all x1, waiting for transfers between devices, body(): lax.all_to_all(send_numerator, 'req', split_axis=0, concat_axis=0, tiled=...  450 us
    psum x1, waiting for transfers between devices, body(): lax.psum(jnp.dot(attention, out_weight, preferred_element_type=jnp.float3...  102 us
    all_gather x1, waiting for transfers between devices, body(): everyone = lax.all_gather(query, 'req', axis=0, tiled=True)  81.2 us
    reshape x1, local copies, waits for them, and re-layouts, body(): send_numerator = jnp.concatenate([pre_numerator, request_numerator.reshap...  35.5 us
  transfers between devices with their start and end apart: 5, of which 3 were waited for; matrix products, arithmetic and copies ran while one was open for 11% of the time, Pallas kernels for 0%

commit v1 on v0

--- a/solution.py
+++ b/solution.py
@@ -1,7 +1,9 @@
+import functools
 import jax
 import jax.numpy as jnp
 from jax import lax
 from jax.sharding import PartitionSpec as P
+from jax.lax import all_gather
 
 HD = 128
 SPAN = 288
@@ -9,6 +11,13 @@
 EPSILON = 1e-06
 THETA = 500000.0
 NEGATIVE = -1e30
+
+
+def matrix_write(s0, which_axis):
+    return jnp.sum(all_gather(s0, axis_name=which_axis), axis=0)
+
+
+obtain_the_packet = functools.partial(matrix_write, which_axis="tp")
 
 
 def rotate(values, positions):
@@ -175,7 +184,9 @@
     )
     attention = merged.reshape(rows_group, local_width).astype(jnp.bfloat16)
     share_width = post_gain.shape[0]
-    projected = lax.psum(jnp.dot(attention, out_weight, preferred_element_type=jnp.float32), "tp")
+    projected = obtain_the_packet(
+        jnp.dot(attention, out_weight, preferred_element_type=jnp.float32)
+    )
     inverse = lax.rsqrt(jnp.mean(projected * projected, 1) + EPSILON)
     my_share = lax.dynamic_slice_in_dim(projected, tp_index * share_width, share_width, 1)
     normed = my_share * inverse[:, None]

time: 843 us -> 1010 us (1.20)
  waiting for transfers between devices: 633 us -> 768 us
  other arithmetic: 46.9 us -> 73.5 us
    all_gather x0 -> x1, waiting for transfers between devices: none -> 233 us  [matrix_write(): return jnp.sum(all_gather(s0, axis_name=which_axis), axis=0)]
    psum x1 -> x0, waiting for transfers between devices: 102 us -> none  [body(): lax.psum(jnp.dot(attention, out_weight, preferred_element_type=jnp.float3...]
    reduce_sum x0 -> x1, other arithmetic: none -> 26.4 us  [matrix_write(): return jnp.sum(all_gather(s0, axis_name=which_axis), axis=0)]
  transfers between devices with their start and end apart: 5 -> 5, of which waited for: 3 -> 3; matrix products, arithmetic and copies ran while one was open for 11% -> 10% of each run, Pallas kernels for 0% -> 0%
where the time goes in v1:
time: 1010 us; the launch traced here: 1000 us
  waiting for transfers between devices  768 us (76%)
  local copies, waits for them, and re-layouts  75.1 us (7%)
  other arithmetic  73.5 us (7%)
  matrix products  34 us (3%)
  starting transfers between devices  24.5 us (2%)
  blocking collectives  15 us (1%)
  between operations  13.8 us (1%)
    all_to_all x1, waiting for transfers between devices, body(): lax.all_to_all(send_numerator, 'req', split_axis=0, concat_axis=0, tiled=...  454 us
    all_gather x1, waiting for transfers between devices, matrix_write(): return jnp.sum(all_gather(s0, axis_name=which_axis), axis=0)  233 us
    all_gather x1, waiting for transfers between devices, body(): everyone = lax.all_gather(query, 'req', axis=0, tiled=True)  81.2 us
    reshape x1, local copies, waits for them, and re-layouts, body(): send_numerator = jnp.concatenate([pre_numerator, request_numerator.reshap...  35.5 us
    reduce_sum x1, other arithmetic, matrix_write(): return jnp.sum(all_gather(s0, axis_name=which_axis), axis=0)  26.4 us
  transfers between devices with their start and end apart: 5, of which 3 were waited for; matrix products, arithmetic and copies ran while one was open for 10% of the time, Pallas kernels for 0%

profile of v1, /device:TPU:1, one launch (start us, length us, event | category | flops | bytes accessed | tf_op | source)
XLA Modules:
  0.0 1004.1 jit_solution(1491034992551088360)
XLA Ops:
  6.6 1.2 dynamic_slice.9
  7.8 0.6 iota_add_fusion
  8.5 1.1 fusion.22
  9.5 1.1 fusion.24
  10.6 15.0 %all-reduce.1 = (f32[296]{0:T(512)S(1)}, f32[296]{0:T(512)S(1)}) all-reduce(f32[296]{0:T(512)S(1)} %fusion.24, f32[296]{0:T(512)S(1)} %fusion.22), channel_id=1, replica_groups=mesh['req'=32,'tp'=8] {'tp'}, use_global_device_ids=true, to_apply=%region_6.7 | all-reduce | flops 592 | bytes 4736 | tf_op jit(solution)/shard_map/psum | solution.py:89
  25.6 1.1 fusion.25
  26.7 0.2 reshape.278
  26.9 1.0 fusion.23
  27.9 0.2 reshape.272
  28.1 1.4 fusion.74
  29.5 1.5 fusion.75
  31.0 0.1 dynamic_slice.10
  31.1 0.1 add_convert_fusion.3
  31.1 0.6 multiply_cosine_fusion
  31.7 2.8 subtract_convert_fusion.1
  34.6 0.7 copy-done.4
  35.2 0.1 copy-done.6
  35.3 0.8 pad_maximum_fusion.3
  36.2 0.6 gather_fusion
  36.8 2.3 copy.97
  39.2 2.3 copy.104
  41.5 2.9 copy.94
  44.4 3.5 copy.102
  48.0 0.1 fusion.62
  48.1 81.2 %all-gather.4.cloned.1.call-done = bf16[9472,3,128]{2,0,1:T(8,128)(2,1)} async-done(((bf16[296,3,128]{2,0,1:T(8,128)(2,1)}), bf16[9472,3,128]{2,0,1:T(8,128)(2,1)}) %all-gather.4.cloned.1.call-update) | async-done | bytes 7274512 | tf_op jit(solution)/shard_map/all_gather | solution.py:120
  129.3 0.9 slice_bitcast_fusion.1
  130.3 0.2 copy.96
  130.5 0.6 gather_fusion.1
  131.0 1.4 fusion.47
  132.5 0.1 fusion.59
  132.6 0.8 fusion.57
  133.3 0.1 select_reduce_fusion
  133.4 0.1 reshape.277
  133.6 1.6 fusion.45
  135.2 1.3 convolution_bitcast_fusion.2
  136.5 14.0 %bitcast_reduce_fusion = (f32[32,288,3]{1,2,0:T(4,128)S(1)}, f32[32,3,288,128]{3,2,1,0:T(8,128)}) fusion(pred[32,128]{1,0:T(8,128)(4,1)S(1)} %broadcast_compare_fusion, bf16[32,128,3,128]{1,3,2,0:T(8,128)(2,1)} %bitcast.98, bf16[32,296,3,128]{3,1,0,2:T(8,128)(2,1)} %bitcast.104), kind=kOutput, calls=%fused_computation.6 | convolution fusion | flops 916558848 | bytes 24494080 | tf_op jit(solution)/shard_map/gqhd,gkhd->gqhk/dot_general | solution.py:130
  150.5 0.8 pad_maximum_fusion.1
  151.3 5.8 all-to-all-start
  157.1 11.9 %fusion.3 = f32[32,288,3]{1,2,0:T(4,128)} fusion(f32[32,3,288,128]{3,2,1,0:T(8,128)} %get-tuple-element.28, f32[32,288,3]{1,2,0:T(4,128)S(1)} %get-tuple-element.27, pred[32,128]{1,0:T(8,128)(4,1)S(1)} %broadcast_compare_fusion), kind=kLoop, calls=%fused_computation.10 | loop fusion | flops 17667072 | bytes 14381056 | tf_op jit(solution)/shard_map/reduce_sum | solution.py:40
  169.0 10.0 convolution_bitcast_fusion
  179.0 0.2 fusion.41
  179.2 0.1 reshape.284
  179.4 1.2 copy.105
  180.5 1.7 pad_maximum_fusion.2
  182.2 9.0 all-to-all-start.2
  191.3 11.2 %pad_maximum_fusion = f32[32,296,3,128]{3,1,2,0:T(8,128)} fusion(f32[32,288,3,128]{3,1,2,0:T(8,128)} %convolution_bitcast_fusion, f32[256,3,128]{2,0,1:T(8,128)S(1)} %copy.105), kind=kLoop, calls=%fused_computation.4 | loop fusion | flops 3637248 | bytes 29097984 | tf_op jit(solution)/shard_map/concatenate | solution.py:165
  202.4 11.1 %copy.107 = f32[32,296,3,128]{3,1,0,2:T(8,128)} copy(f32[32,296,3,128]{3,1,2,0:T(8,128)} %pad_maximum_fusion) | data formatting | bytes 29097984 | tf_op jit(solution)/shard_map/concatenate | solution.py:165
  213.6 35.5 %copy.108 = f32[9472,3,128]{2,1,0:T(4,128)} copy(f32[9472,3,128]{2,0,1:T(8,128)} %bitcast.95) | data formatting | bytes 29097984 | tf_op jit(solution)/shard_map/reshape | solution.py:167
  249.1 9.5 all-to-all-start.1
  258.6 0.3 all-gather.6.cloned.1.call-start
  258.9 0.2 multiply_reduce_fusion.1
  259.1 0.5 fusion.76
  259.6 0.3 fusion.16
  259.9 0.5 convolution_bitcast_fusion.1
  260.5 0.1 fusion.64
  260.6 0.1 fusion.38
  260.8 453.6 %all-to-all-done.1 = f32[9472,3,128]{2,1,0:T(4,128)} async-done(((f32[9472,3,128]{2,1,0:T(4,128)}), f32[9472,3,128]{2,1,0:T(4,128)}, u32[]{:S(2)}, u32[]{:S(2)}) %all-to-all-start.1) | async-done | bytes 14549024 | tf_op jit(solution)/shard_map/all_to_all | solution.py:171
  714.4 8.4 copy.111
  722.7 4.9 fusion
  727.7 4.4 fusion.26
  732.2 233.4 %all-gather.6.cloned.1.call-done = f32[2368,5120]{1,0:T(8,128)} async-done(((f32[296,5120]{1,0:T(8,128)}), f32[2368,5120]{1,0:T(8,128)}) %all-gather.6.cloned.1.call-update) | async-done | bytes 48496656 | tf_op jit(solution)/shard_map/all_gather | solution.py:17
  965.5 26.4 %reduce_sum.98 = f32[296,5120]{1,0:T(8,128)} reduce(f32[8,296,5120]{2,1,0:T(8,128)} %bitcast.96, f32[]{:T(128)} %constant.23.clone.1), dimensions={0}, to_apply=%region_15.16 | reduce | flops 10608640 | bytes 54558724 | tf_op jit(solution)/shard_map/reduce_sum | solution.py:17
  992.0 3.2 multiply_reduce_fusion
  995.2 2.1 add_convert_fusion
  (57 shorter events, 0.5 us)
Async XLA Ops:
  6.5 24.5 %copy-start = (s32[256]{0:T(256)S(1)}, s32[256]{0:T(256)}, u32[]{:S(2)}) copy-start(s32[256]{0:T(256)} %param.30) | copy-start | bytes 3076
  6.5 29.6 %copy-start.13 = (s32[8]{0:T(128)S(1)}, s32[8]{0:T(128)}, u32[]{:S(2)}) copy-start(s32[8]{0:T(128)} %param.28) | copy-start | bytes 100
  6.5 122.8 %all-gather.4.cloned.1.call-start = ((), (), s32[]{:S(2)}) async-start(), calls=%async_computation.3 | async-start | bytes 7501824 | tf_op jit(solution)/shard_map/all_gather | solution.py:120
  31.0 10.5 %copy-start.3 = (bf16[32,1,128,384]{3,2,1,0:T(8,128)(2,1)S(1)}, bf16[32,1,128,384]{3,2,1,0:T(8,128)(2,1)}, u32[]{:S(2)}) copy-start(bf16[32,1,128,384]{3,2,1,0:T(8,128)(2,1)} %param.24) | copy-start | bytes 9437188
  34.6 0.7 copy-start.4
  34.6 0.8 copy-start.6
  39.2 8.7 copy-start.16
  39.2 8.9 copy-start.14
  151.3 30.9 %all-to-all-start = ((f32[32,296,3]{1,2,0:T(4,128)}), f32[32,296,3]{1,2,0:T(4,128)S(1)}, u32[]{:S(2)}, u32[]{:S(2)}) async-start(f32[32,296,3]{1,2,0:T(4,128)} %pad_maximum_fusion.1), calls=%async_computation | async-start | bytes 393216 | tf_op jit(solution)/shard_map/all_to_all | solution.py:169
  157.0 11.9 %copy-start.1 = (f32[32,3,288,128]{3,2,1,0:T(8,128)S(1)}, f32[32,3,288,128]{3,2,1,0:T(8,128)}, u32[]{:S(2)}) copy-start(f32[32,3,288,128]{3,2,1,0:T(8,128)} %get-tuple-element.28) | copy-start | bytes 42467332
  169.0 10.0 copy-start.12
  182.2 66.9 %all-to-all-start.2 = ((f32[32,296,3]{1,2,0:T(4,128)}), f32[32,296,3]{1,2,0:T(4,128)S(1)}, u32[]{:S(2)}, u32[]{:S(2)}) async-start(f32[32,296,3]{1,2,0:T(4,128)} %pad_maximum_fusion.2), calls=%async_computation.2 | async-start | bytes 393216 | tf_op jit(solution)/shard_map/all_to_all | solution.py:170
  249.1 9.8 copy-start.5
  249.1 9.8 copy-start.7
  249.1 9.8 copy-start.8
  249.1 9.8 copy-start.9
  249.1 10.8 %copy-start.15 = (bf16[296,384]{1,0:T(8,128)(2,1)S(1)}, bf16[296,384]{1,0:T(8,128)(2,1)}, u32[]{:S(2)}) copy-start(bf16[296,384]{1,0:T(8,128)(2,1)} %param.19) | copy-start | bytes 681988
  249.1 465.3 %all-to-all-start.1 = ((f32[9472,3,128]{2,1,0:T(4,128)}), f32[9472,3,128]{2,1,0:T(4,128)}, u32[]{:S(2)}, u32[]{:S(2)}) async-start(f32[9472,3,128]{2,1,0:T(4,128)} %copy.108), calls=%async_computation.1 | async-start | bytes 38797312 | tf_op jit(solution)/shard_map/all_to_all | solution.py:171
  258.6 706.9 %all-gather.6.cloned.1.call-start = ((), (), s32[]{:S(2)}) async-start(), calls=%async_computation.4 | async-start | bytes 54558720 | tf_op jit(solution)/shard_map/all_gather | solution.py:17
  722.7 5.0 copy-start.2
  965.5 29.7 %copy-start.10 = (bf16[296,640]{1,0:T(8,128)(2,1)S(1)}, bf16[296,640]{1,0:T(8,128)(2,1)}, u32[]{:S(2)}) copy-start(bf16[296,640]{1,0:T(8,128)(2,1)} %param.16) | copy-start | bytes 1136644
  965.5 29.7 %copy-start.11 = (f32[640]{0:T(1024)S(1)}, f32[640]{0:T(1024)}, u32[]{:S(2)}) copy-start(f32[640]{0:T(1024)} %param.23) | copy-start | bytes 7684
Sparse Core Ops, SparseCore 0:
  36.3 93.0 all-gather.3
  732.3 233.1 all-gather.5
